TPU v7x, 512 devices: a whole 4x4x16 slice. The times are simulated.
512 devices in a mesh: case: 8 (over x, core), elem: 64 (over y, z).
Axes of the slice: x: 4, y: 4, z: 16, core: 2. Of those that a mesh axis runs over, the one named last changes fastest.
Arguments:
- load_coef: bfloat16 [4096, 512], P(('case', 'elem')), may hold values from -13 to 13
- mantissa: bfloat16 [512, 3, 65536], P(None, None, 'elem'), may hold values from -0.25 to 0.25
- scale_exp: int32 [512, 3, 512], P(None, None, 'elem'), may hold values from -1 to 1
- lin_coef: float32 [2, 65536], P(None, 'elem'), may hold values from -0.5 to 0.5
- quad_coef: float32 [3, 65536], P(None, 'elem'), may hold values from 0.05 to 0.3
- cross_coef: float32 [65536], P('elem'), may hold values from -0.1 to 0.1
- ply_count: int32 [65536], P('elem'), may hold values from 0 to 7
- cotangent: float32 [4096], P('case'), may hold values from -6 to 6
Outputs:
- load_grad: float32 [4096, 512], P(('case', 'elem'))
- coef_grad: float32 [6, 65536], P(None, 'elem')
All inputs are finite; a program needn't handle non-finite values.
Results may differ from a plain program's by a relative error of at most 0.0065.
Values may be sent and summed in bfloat16 or wider, within the bound.
A program may use at most 64 MiB of HBM per device.

v0:
```python
import jax
import jax.numpy as jnp
from jax import lax
from jax.sharding import PartitionSpec as P

rho_value = 1.0


def per_device(
    load_coef, mantissa, scale_exp, lin_coef, quad_coef, cross_coef, ply_count, cotangent
):
    units, comps, width = mantissa.shape
    blocks = scale_exp.shape[2]
    factor = jnp.exp2(scale_exp.astype(jnp.float32)).astype(jnp.bfloat16)
    fields = (mantissa.reshape(units, comps, blocks, width // blocks) * factor[..., None]).reshape(
        units, comps * width
    )
    stress = jnp.dot(
        lax.all_gather(load_coef, "elem", axis=0, tiled=True),
        fields,
        preferred_element_type=jnp.float32,
    )
    first = stress[:, :width]
    second = stress[:, width : 2 * width]
    shear = stress[:, 2 * width :]
    plies = (ply_count + 1).astype(jnp.float32)
    index = (
        lin_coef[0] * first
        + lin_coef[1] * second
        + quad_coef[0] * first * first
        + quad_coef[1] * second * second
        + quad_coef[2] * shear * shear
        + 2.0 * cross_coef * first * second
    )
    local_peak = jnp.max(index, axis=1)
    peak = lax.pmax(local_peak, "elem")
    local_total = jnp.sum(plies * jnp.exp(rho_value * (index - peak[:, None])), axis=1)
    total = lax.psum(local_total, "elem")
    envelope = peak + jnp.log(total) / rho_value
    weight = cotangent[:, None] * plies * jnp.exp(rho_value * (index - envelope[:, None]))
    grad_one = weight * (lin_coef[0] + 2.0 * quad_coef[0] * first + 2.0 * cross_coef * second)
    grad_two = weight * (lin_coef[1] + 2.0 * quad_coef[1] * second + 2.0 * cross_coef * first)
    grad_three = weight * (2.0 * quad_coef[2] * shear)
    dstress = jnp.concatenate([grad_one, grad_two, grad_three], axis=1).astype(jnp.bfloat16)
    coef_local = jnp.stack(
        [
            jnp.sum(weight * first, axis=0),
            jnp.sum(weight * second, axis=0),
            jnp.sum(weight * first * first, axis=0),
            jnp.sum(weight * second * second, axis=0),
            jnp.sum(weight * shear * shear, axis=0),
            jnp.sum(weight * 2.0 * first * second, axis=0),
        ]
    )
    terms = lax.dot_general(
        dstress, fields, (((1,), (1,)), ((), ())), preferred_element_type=jnp.float32
    )
    load_grad = lax.psum_scatter(terms, "elem", scatter_dimension=0, tiled=True)
    coef_grad = lax.psum(coef_local, "case")
    return (load_grad, coef_grad)


def solution(mesh):
    return jax.shard_map(
        per_device,
        mesh=mesh,
        in_specs=(
            P(("case", "elem"), None),
            P(None, None, "elem"),
            P(None, None, "elem"),
            P(None, "elem"),
            P(None, "elem"),
            P("elem"),
            P("elem"),
            P("case"),
        ),
        out_specs=(P(("case", "elem"), None), P(None, "elem")),
        check_vma=False,
    )
```

profile of v0, /device:TPU:2, one launch (start us, length us, event | category | flops | bytes accessed | tf_op | source)
XLA Modules:
  0.0 1110.7 jit_solution(16444660311962095111)
XLA Ops:
  7.2 0.0 reduce-scatter.2.cloned.1.call-start
  7.2 0.7 broadcast_multiply_fusion.3
  7.9 0.7 add_convert_fusion
  8.6 0.8 fusion.14
  9.4 0.8 exponential_convert_fusion
  10.2 0.9 broadcast_multiply_fusion.2
  11.0 114.9 %all_gather.3 = bf16[512,512]{1,0:T(8,128)(2,1)} all-gather(bf16[8,512]{1,0:T(8,128)(2,1)} %param.8), channel_id=1, replica_groups=mesh['case'=8,'elem'=64] {'elem'}, dimensions={0}, use_global_device_ids=true | all-gather | bytes 532480 | tf_op jit(solution)/shard_map/all_gather | solution.py:19
  125.9 3.2 copy.11
  129.1 0.0 copy-start.3
  129.1 0.4 bitcast_multiply_fusion
  129.6 0.6 copy-done.3
  130.2 0.0 copy-start.1
  130.2 1.8 convolution_bitcast_fusion
  132.0 0.0 copy-done.1
  132.0 0.0 copy-start
  132.0 1.4 fusion.12
  133.5 1.2 copy-done
  134.7 0.0 copy-start.4
  134.7 140.5 %pmax.7 = f32[512]{0:T(512)S(1)} all-reduce(f32[512]{0:T(512)S(1)} %get-tuple-element.8), channel_id=1, replica_groups=mesh['case'=8,'elem'=64] {'elem'}, use_global_device_ids=true, to_apply=%region_1.0 | all-reduce | flops 512 | bytes 4096 | tf_op jit(solution)/shard_map/pmax | solution.py:36
  275.1 0.5 multiply_reduce_fusion.3
  275.7 138.0 %psum.14 = f32[512]{0:T(512)S(1)} all-reduce(f32[512]{0:T(512)S(1)} %multiply_reduce_fusion.3), channel_id=1, replica_groups=mesh['case'=8,'elem'=64] {'elem'}, use_global_device_ids=true, to_apply=%region_3.0 | all-reduce | flops 512 | bytes 4096 | tf_op jit(solution)/shard_map/psum | solution.py:38
  413.7 0.0 copy-done.4
  413.7 0.0 copy-start.2
  413.7 4.8 multiply_reduce_fusion
  418.5 0.0 copy-done.2
  418.5 2.8 fusion
  421.3 0.0 reduce-scatter.2.cloned.1.call-update
  421.3 0.1 stack.27
  421.3 21.3 %psum.15 = f32[6,1024]{1,0:T(8,128)} all-reduce(f32[6,1024]{1,0:T(8,128)S(1)} %stack.27), channel_id=1, replica_groups=mesh['case'=8,'elem'=64] {'case'}, use_global_device_ids=true, to_apply=%region_11.0 | all-reduce | flops 6144 | bytes 49152 | tf_op jit(solution)/shard_map/psum | solution.py:59
  442.6 661.3 %reduce-scatter.2.cloned.1.call-done = f32[8,512]{1,0:T(8,128)} async-done(((f32[512,512]{1,0:T(8,128)}), f32[8,512]{1,0:T(8,128)}) %reduce-scatter.2.cloned.1.call-update) | async-done | bytes 16400 | tf_op jit(solution)/shard_map/reduce_scatter | solution.py:58
  (1 shorter events, 0.0 us)
Async XLA Ops:
  7.2 1096.7 %reduce-scatter.2.cloned.1.call-start = ((), (), s32[]{:S(2)}) async-start(), calls=%async_computation.1 | async-start | bytes 1064960 | tf_op jit(solution)/shard_map/reduce_scatter | solution.py:58
  129.1 1.0 copy-start.3
  130.2 1.8 copy-start.1
  132.0 2.7 copy-start
  134.7 279.0 %copy-start.4 = (f32[512]{0:T(512)S(1)}, f32[512]{0:T(512)}, u32[]{:S(2)}) copy-start(f32[512]{0:T(512)} %param.15) | copy-start | bytes 6148
  413.7 4.8 copy-start.2
Sparse Core Ops, SparseCore 0:
  421.4 682.4 reduce-scatter.1
where the time goes:
time: 1110 us
  waiting for transfers between devices  661 us (60%)
  blocking collectives  415 us (37%)
  between operations  14.1 us (1%)
    reduce_scatter x1, waiting for transfers between devices, per_device(): load_grad = lax.psum_scatter(terms, 'elem', scatter_dimension=0, tiled=True)  661 us
    pmax x1, blocking collectives, per_device(): peak = lax.pmax(local_peak, 'elem')  140 us
    psum x1, blocking collectives, per_device(): total = lax.psum(local_total, 'elem')  138 us
    all_gather x1, blocking collectives, per_device(): lax.all_gather(load_coef, 'elem', axis=0, tiled=True)  115 us
  transfers between devices with their start and end apart: 1, of which 1 were waited for; matrix products, arithmetic and copies ran while one was open for 0% of the time, Pallas kernels for 0%

commit v1 on v0

--- a/solution.py
+++ b/solution.py
@@ -16,7 +16,9 @@
         units, comps * width
     )
     stress = jnp.dot(
-        lax.all_gather(load_coef, "elem", axis=0, tiled=True),
+        jnp.concatenate(
+            lax.all_to_all(jnp.stack([load_coef] * lax.axis_size("elem")), "elem", 0, 0), axis=0
+        ),
         fields,
         preferred_element_type=jnp.float32,
     )

time: 1110 us -> 1040 us (0.937)
  blocking collectives: 415 us -> 299 us
  waiting for transfers between devices: 661 us -> 685 us
  starting transfers between devices: 0.04 us -> 19 us
    all_gather x1 -> x0, blocking collectives: 115 us -> none  [per_device(): lax.all_gather(load_coef, 'elem', axis=0, tiled=True)]
    all_to_all x0 -> x1, waiting for transfers between devices: none -> 24.2 us  [per_device(): lax.all_to_all(jnp.stack([load_coef] * lax.axis_size('elem')), 'elem', 0, 0)]
    all_to_all x0 -> x1, starting transfers between devices: none -> 19 us  [per_device(): lax.all_to_all(jnp.stack([load_coef] * lax.axis_size('elem')), 'elem', 0, 0)]
  transfers between devices with their start and end apart: 1 -> 2, of which waited for: 1 -> 2; matrix products, arithmetic and copies ran while one was open for 0% -> 1% of each run, Pallas kernels for 0% -> 0%
where the time goes in v1:
time: 1040 us
  waiting for transfers between devices  685 us (66%)
  blocking collectives  299 us (29%)
  starting transfers between devices  19 us (2%)
  between operations  14.1 us (1%)
  other arithmetic  10.8 us (1%)
    reduce_scatter x1, waiting for transfers between devices, per_device(): load_grad = lax.psum_scatter(terms, 'elem', scatter_dimension=0, tiled=True)  660 us
    pmax x1, blocking collectives, per_device(): peak = lax.pmax(local_peak, 'elem')  139 us
    psum x1, blocking collectives, per_device(): total = lax.psum(local_total, 'elem')  139 us
    all_to_all x1, waiting for transfers between devices, per_device(): lax.all_to_all(jnp.stack([load_coef] * lax.axis_size('elem')), 'elem', 0, 0)  24.2 us
    psum x1, blocking collectives, per_device(): coef_grad = lax.psum(coef_local, 'case')  21.3 us
  transfers between devices with their start and end apart: 2, of which 2 were waited for; matrix products, arithmetic and copies ran while one was open for 1% of the time, Pallas kernels for 0%

profile of v1, /device:TPU:2, one launch (start us, length us, event | category | flops | bytes accessed | tf_op | source)
XLA Modules:
  0.0 1040.5 jit_solution(5137413751370461217)
XLA Ops:
  7.2 1.5 stack.16
  8.7 19.0 %all-to-all-start = ((bf16[64,8,512]{2,1,0:T(8,128)(2,1)}), bf16[64,8,512]{2,1,0:T(8,128)(2,1)}, u32[]{:S(2)}, u32[]{:S(2)}) async-start(bf16[64,8,512]{2,1,0:T(8,128)(2,1)} %stack.16), calls=%async_computation | async-start | bytes 1048576 | tf_op jit(solution)/shard_map/all_to_all | solution.py:20
  27.7 0.0 copy-start.2
  27.7 0.0 reduce-scatter.2.cloned.1.call-start
  27.8 3.2 copy.11
  31.0 0.0 copy-done.2
  31.0 2.1 bitcast_multiply_fusion
  33.1 0.0 copy-start.5
  33.1 0.0 copy-start.6
  33.1 0.0 copy-start.4
  33.1 0.0 copy-start.3
  33.1 1.9 bitcast_multiply_fusion.1
  35.0 0.0 copy-done.5
  35.0 0.0 copy-done.6
  35.0 0.0 copy-done.4
  35.1 0.0 copy-done.3
  35.1 24.2 %all-to-all-done = bf16[64,8,512]{2,1,0:T(8,128)(2,1)} async-done(((bf16[64,8,512]{2,1,0:T(8,128)(2,1)}), bf16[64,8,512]{2,1,0:T(8,128)(2,1)}, u32[]{:S(2)}, u32[]{:S(2)}) %all-to-all-start) | async-done | bytes 524320 | tf_op jit(solution)/shard_map/all_to_all | solution.py:20
  59.3 3.8 convolution_bitcast_fusion
  63.1 0.0 copy-start
  63.1 1.4 fusion.13
  64.5 1.2 copy-done
  65.7 139.4 %pmax.7 = f32[512]{0:T(512)S(1)} all-reduce(f32[512]{0:T(512)S(1)} %get-tuple-element.8), channel_id=1, replica_groups=mesh['case'=8,'elem'=64] {'elem'}, use_global_device_ids=true, to_apply=%region_1.0 | all-reduce | flops 512 | bytes 4096 | tf_op jit(solution)/shard_map/pmax | solution.py:38
  205.1 0.5 multiply_reduce_fusion.3
  205.6 138.6 %psum.14 = f32[512]{0:T(512)S(1)} all-reduce(f32[512]{0:T(512)S(1)} %multiply_reduce_fusion.3), channel_id=1, replica_groups=mesh['case'=8,'elem'=64] {'elem'}, use_global_device_ids=true, to_apply=%region_3.0 | all-reduce | flops 512 | bytes 4096 | tf_op jit(solution)/shard_map/psum | solution.py:40
  344.2 0.0 copy-done.7
  344.2 4.8 multiply_reduce_fusion
  349.0 0.0 copy-done.1
  349.0 2.8 fusion
  351.8 0.0 reduce-scatter.2.cloned.1.call-update
  351.8 0.1 stack.23
  351.9 21.3 %psum.15 = f32[6,1024]{1,0:T(8,128)} all-reduce(f32[6,1024]{1,0:T(8,128)S(1)} %stack.23), channel_id=1, replica_groups=mesh['case'=8,'elem'=64] {'case'}, use_global_device_ids=true, to_apply=%region_11.0 | all-reduce | flops 6144 | bytes 49152 | tf_op jit(solution)/shard_map/psum | solution.py:61
  373.1 660.5 %reduce-scatter.2.cloned.1.call-done = f32[8,512]{1,0:T(8,128)} async-done(((f32[512,512]{1,0:T(8,128)}), f32[8,512]{1,0:T(8,128)}) %reduce-scatter.2.cloned.1.call-update) | async-done | bytes 16400 | tf_op jit(solution)/shard_map/reduce_scatter | solution.py:60
  (8 shorter events, 0.1 us)
Async XLA Ops:
  8.7 50.6 %all-to-all-start = ((bf16[64,8,512]{2,1,0:T(8,128)(2,1)}), bf16[64,8,512]{2,1,0:T(8,128)(2,1)}, u32[]{:S(2)}, u32[]{:S(2)}) async-start(bf16[64,8,512]{2,1,0:T(8,128)(2,1)} %stack.16), calls=%async_computation | async-start | bytes 1048576 | tf_op jit(solution)/shard_map/all_to_all | solution.py:20
  27.7 3.3 copy-start.2
  27.7 1005.9 %reduce-scatter.2.cloned.1.call-start = ((), (), s32[]{:S(2)}) async-start(), calls=%async_computation.2 | async-start | bytes 1064960 | tf_op jit(solution)/shard_map/reduce_scatter | solution.py:60
  33.1 1.9 copy-start.5
  33.1 1.9 copy-start.6
  33.1 1.9 copy-start.4
  33.1 1.9 copy-start.3
  63.1 2.7 copy-start
  65.7 278.5 %copy-start.7 = (f32[512]{0:T(512)S(1)}, f32[512]{0:T(512)}, u32[]{:S(2)}) copy-start(f32[512]{0:T(512)} %param.15) | copy-start | bytes 6148
  344.2 4.8 copy-start.1
Sparse Core Ops, SparseCore 0:
  352.0 681.6 reduce-scatter.1
